TPU v7x, 256 devices: a whole 4x4x8 slice. The times are simulated.
256 devices in a mesh: orb: 8 (over x, core), dom: 32 (over y, z).
Axes of the slice: x: 4, y: 4, z: 8, core: 2. Of those that a mesh axis runs over, the one named last changes fastest.
Arguments:
- orbitals: float32 [768, 128, 8, 128], P('orb', 'dom'), may hold values from -6 to 6
- potential: float32 [128, 8, 128], P('dom'), may hold values from -1 to 3
- prev_gradient: float32 [768, 128, 8, 128], P('orb', 'dom'), may hold values from -24 to 24
- prev_direction: float32 [768, 128, 8, 128], P('orb', 'dom'), may hold values from -24 to 24
Outputs:
- new_orbitals: float32 [768, 128, 8, 128], P('orb', 'dom')
- new_direction: float32 [768, 128, 8, 128], P('orb', 'dom')
- gradient: float32 [768, 128, 8, 128], P('orb', 'dom')
All inputs are finite; a program needn't handle non-finite values.
Results may differ from a plain program's by a relative error of at most 0.0002.
Values sent between devices are 32-bit elements; how exact they have to be, the bound alone decides.
No kernel may reach another device: no remote copies, remote signals or barrier semaphores. Data moves between devices by JAX's collectives and lax.ppermute only.
A program may use at most 128 MiB of HBM per device.

v0:
```python
import jax
import jax.numpy as jnp
from jax import lax
from jax.sharding import PartitionSpec as P

coeffs = (-205.0 / 72.0, 8.0 / 5.0, -1.0 / 5.0, 8.0 / 315.0, -1.0 / 560.0)
step_length = 0.05


def padded_2(cells, sides, width):
    for axis, dim in sides:
        count = lax.axis_size(axis)
        ends = count - 1
        head = lax.slice_in_dim(cells, 0, width, axis=dim)
        tail = lax.slice_in_dim(cells, cells.shape[dim] - width, cells.shape[dim], axis=dim)
        cells = jnp.concatenate(
            [
                lax.ppermute(tail, axis, [(i, (i + 1) % count) for i in range(ends)]),
                cells,
                lax.ppermute(head, axis, [((i + 1) % count, i) for i in range(ends)]),
            ],
            axis=dim,
        )
    return cells


def laplace(padded, planes, lines, columns):
    center = padded[:, 4 : 4 + planes, 4 : 4 + lines, 4 : 4 + columns]
    total = 3.0 * coeffs[0] * center
    for offset in range(1, 5):
        total = total + coeffs[offset] * (
            padded[:, 4 + offset : 4 + offset + planes, 4 : 4 + lines, 4 : 4 + columns]
            + padded[:, 4 - offset : 4 - offset + planes, 4 : 4 + lines, 4 : 4 + columns]
        )
        total = total + coeffs[offset] * (
            padded[:, 4 : 4 + planes, 4 + offset : 4 + offset + lines, 4 : 4 + columns]
            + padded[:, 4 : 4 + planes, 4 - offset : 4 - offset + lines, 4 : 4 + columns]
        )
        total = total + coeffs[offset] * (
            padded[:, 4 : 4 + planes, 4 : 4 + lines, 4 + offset : 4 + offset + columns]
            + padded[:, 4 : 4 + planes, 4 : 4 + lines, 4 - offset : 4 - offset + columns]
        )
    return total


def highdot(left, right):
    return jnp.dot(left, right, precision=lax.Precision.HIGHEST, preferred_element_type=jnp.float32)


def on_device(orbitals, potential, prev_gradient, prev_direction):
    block = orbitals.shape[0]
    extended = padded_2(orbitals, (("dom", 1),), 4)
    padded = jnp.pad(extended, ((0, 0), (0, 0), (4, 4), (4, 4)))
    lap = laplace(padded, orbitals.shape[1], orbitals.shape[2], orbitals.shape[3])
    image = -0.5 * lap + potential[None] * orbitals
    cmat = orbitals.reshape(block, -1)
    hmat_rows = image.reshape(block, -1)
    cells = cmat.shape[1] * lax.axis_size("dom")
    cell_orbs, cell_images = (
        lax.all_to_all(cmat, "orb", split_axis=1, concat_axis=0, tiled=True),
        lax.all_to_all(hmat_rows, "orb", split_axis=1, concat_axis=0, tiled=True),
    )
    correlation, hamilton = lax.psum(
        (highdot(cell_orbs, cell_orbs.T), highdot(cell_orbs, cell_images.T)), ("orb", "dom")
    )
    correlation = correlation / cells
    hamilton = hamilton / cells
    cell_grad = (
        4.0 * cell_images
        - 2.0 * highdot(correlation.T, cell_images)
        - 2.0 * highdot(hamilton.T, cell_orbs)
    )
    grad = lax.all_to_all(cell_grad, "orb", split_axis=0, concat_axis=1, tiled=True)
    grad = grad.reshape(orbitals.shape)
    both, cross, before = lax.psum(
        (
            jnp.sum(grad * grad),
            jnp.sum(grad * prev_gradient),
            jnp.sum(prev_gradient * prev_gradient),
        ),
        ("orb", "dom"),
    )
    beta = (both - cross) / before
    direction = -grad + beta * prev_direction
    return (orbitals + step_length * direction, direction, grad)


def solution(mesh):
    in_specs = (
        P("orb", "dom", None, None),
        P("dom", None, None),
        P("orb", "dom", None, None),
        P("orb", "dom", None, None),
    )
    out_specs = (
        P("orb", "dom", None, None),
        P("orb", "dom", None, None),
        P("orb", "dom", None, None),
    )
    return jax.shard_map(
        on_device, mesh=mesh, in_specs=in_specs, out_specs=out_specs, check_vma=False
    )
```

profile of v0, /device:TPU:1, one launch (start us, length us, event | category | flops | bytes accessed | tf_op | source)
XLA Modules:
  0.0 553.9 jit_solution(16415115841045701364)
XLA Ops:
  7.2 5.5 collective-permute-start.1
  15.5 2.1 copy.16
  17.6 5.3 all-to-all-start.1
  22.8 22.1 %collective-permute-done.1 = f32[96,4,8,128]{3,2,1,0:T(8,128)} collective-permute-done((f32[96,4,8,128]{3,2,1,0:T(8,128)}, f32[96,4,8,128]{3,2,1,0:T(8,128)}, u32[]{:S(2)}, u32[]{:S(2)}) %collective-permute-start.1) | collective-permute-done | bytes 1572896 | tf_op jit(solution)/shard_map/ppermute | solution.py:18
  44.9 2.7 constant_dynamic-update-slice_fusion.3
  47.6 2.1 constant_dynamic-update-slice_fusion.1
  49.9 11.4 %select_maximum_fusion = f32[96,12,16,136]{3,2,1,0:T(8,128)} fusion(f32[96,4,8,128]{3,2,1,0:T(8,128)} %collective-permute-done, f32[96,4,8,128]{3,2,1,0:T(8,128)S(1)} %copy-done, f32[96,4,8,128]{3,2,1,0:T(8,128)} %collective-permute-done.1), kind=kLoop, calls=%fused_computation.4 | loop fusion | flops 37601280 | bytes 14745600 | tf_op jit(solution)/shard_map/concatenate | solution.py:16
  61.3 2.8 constant_dynamic-update-slice_fusion
  64.0 41.4 %fusion.10 = f32[96,4,8,128]{3,2,1,0:T(8,128)} fusion(f32[96,12,16,136]{3,2,1,0:T(8,128)} %select_maximum_fusion, f32[96,8,8,128]{3,2,1,0:T(8,128)} %get-tuple-element.13, f32[96,8,8,128]{3,2,1,0:T(8,128)} %constant_dynamic-update-slice_fusion, f32[96,4,8,128]{3,2,1,0:T(8,128)S(1)} %copy-done, f32[96,4,8,128]{3,2,1,0:T(8,128)} %collective-permute-done, ...), kind=kLoop, calls=%fused_computation.18 | loop fusion | flops 15728640 | bytes 40910848 | tf_op jit(solution)/shard_map/add | solution.py:55
  105.5 2.6 all_to_all.40
  108.0 3.5 copy.15
  111.5 6.1 %all-to-all-start = ((f32[96,8,512]{2,0,1:T(8,128)}), f32[96,8,512]{2,0,1:T(8,128)}, u32[]{:S(2)}, u32[]{:S(2)}) async-start(f32[96,8,512]{2,0,1:T(8,128)} %copy.15), calls=%async_computation | async-start | bytes 3145728 | tf_op jit(solution)/shard_map/all_to_all | solution.py:61
  117.6 5.4 fusion.38
  123.0 15.3 %all-to-all-done = f32[96,8,512]{2,0,1:T(8,128)} async-done(((f32[96,8,512]{2,0,1:T(8,128)}), f32[96,8,512]{2,0,1:T(8,128)}, u32[]{:S(2)}, u32[]{:S(2)}) %all-to-all-start) | async-done | bytes 1572896 | tf_op jit(solution)/shard_map/all_to_all | solution.py:61
  138.3 6.8 %convolution_bitcast_fusion = f32[768,768]{1,0:T(8,128)} fusion(f32[768,512]{1,0:T(8,128)} %bitcast.1, f32[768,512]{1,0:T(8,128)S(1)} %bitcast.22), kind=kOutput, calls=%fused_computation.13 | convolution fusion | flops 3623878656 | bytes 5505024 | tf_op jit(solution)/shard_map/dot_general | solution.py:47
  145.1 273.7 %all-reduce.5.cloned.1.call-done = (f32[768,768]{1,0:T(8,128)}, f32[768,768]{1,0:T(8,128)}) async-done(((f32[768,768]{1,0:T(8,128)}, f32[768,768]{1,0:T(8,128)}), (f32[768,768]{1,0:T(8,128)}, f32[768,768]{1,0:T(8,128)})) %all-reduce.5.cloned.1.call-update) | async-done | bytes 4718608 | tf_op jit(solution)/shard_map/psum | solution.py:63
  418.9 5.7 %fusion.3 = f32[768,512]{1,0:T(8,128)S(1)} fusion(f32[768,512]{1,0:T(8,128)S(1)} %bitcast.23, f32[768,768]{1,0:T(8,128)} %get-tuple-element.8), kind=kOutput, calls=%fused_computation.9 | convolution fusion | flops 3624468480 | bytes 5505024 | tf_op jit(solution)/shard_map/dot_general | solution.py:47
  424.6 6.3 %multiply_subtract_fusion = f32[768,512]{1,0:T(8,128)S(1)} fusion(f32[768,512]{1,0:T(8,128)S(1)} %fusion.3, f32[768,512]{1,0:T(8,128)} %bitcast.1, f32[768,768]{1,0:T(8,128)S(1)} %copy-done.1), kind=kOutput, calls=%fused_computation.55 | convolution fusion | flops 3626434560 | bytes 7077888 | tf_op jit(solution)/shard_map/dot_general | solution.py:47
  430.9 27.0 %all_to_all.54 = f32[8,96,512]{2,1,0:T(8,128)S(1)} all-to-all(f32[8,96,512]{2,1,0:T(8,128)S(1)} %bitcast.25), channel_id=1, replica_groups=mesh['orb'=8,'dom'=32] {'orb'}, dimensions={0} | all-to-all | bytes 3145728 | tf_op jit(solution)/shard_map/all_to_all | solution.py:73
  457.9 2.1 copy.18
  459.9 2.4 reshape.24
  462.4 2.9 multiply_reduce_fusion
  466.3 74.7 %all-reduce.1 = (f32[]{:T(128)}, f32[]{:T(128)}, f32[]{:T(128)}) all-reduce(f32[]{:T(128)} %multiply_reduce_fusion.2, f32[]{:T(128)} %get-tuple-element.4, f32[]{:T(128)} %get-tuple-element.3), channel_id=1, replica_groups=mesh['orb'=8,'dom'=32] {'orb','dom'}, use_global_device_ids=true, to_apply=%region_3.4 | all-reduce | flops 3 | bytes 24 | tf_op jit(solution)/shard_map/psum | solution.py:75
  542.9 4.1 multiply_add_fusion
  (13 shorter events, 3.9 us)
Async XLA Ops:
  7.2 37.7 %collective-permute-start.1 = (f32[96,4,8,128]{3,2,1,0:T(8,128)}, f32[96,4,8,128]{3,2,1,0:T(8,128)}, u32[]{:S(2)}, u32[]{:S(2)}) collective-permute-start(f32[96,4,8,128]{3,2,1,0:T(8,128)} %param.4), channel_id=1, source_target_pairs={{0,1},{1,2},{2,3},{3,4},{4,5},{5,6},{6,7},{7,8},{8,9},{9,10},{10,1... | collective-permute-start | bytes 4718600 | tf_op jit(solution)/shard_map/ppermute | solution.py:18
  12.7 37.2 %collective-permute-start = (f32[96,4,8,128]{3,2,1,0:T(8,128)}, f32[96,4,8,128]{3,2,1,0:T(8,128)}, u32[]{:S(2)}, u32[]{:S(2)}) collective-permute-start(f32[96,4,8,128]{3,2,1,0:T(8,128)} %param.4), channel_id=1, source_target_pairs={{1,0},{2,1},{3,2},{4,3},{5,4},{6,5},{7,6},{8,7},{9,8},{10,9},{11,1... | collective-permute-start | bytes 4718600 | tf_op jit(solution)/shard_map/ppermute | solution.py:20
  17.6 93.9 %all-to-all-start.1 = ((f32[96,8,512]{2,0,1:T(8,128)}), f32[96,8,512]{2,0,1:T(8,128)S(1)}, u32[]{:S(2)}, u32[]{:S(2)}) async-start(f32[96,8,512]{2,0,1:T(8,128)} %copy.16), calls=%async_computation.1 | async-start | bytes 3145728 | tf_op jit(solution)/shard_map/all_to_all | solution.py:60
  22.8 24.8 %copy-start = (f32[96,4,8,128]{3,2,1,0:T(8,128)S(1)}, f32[96,4,8,128]{3,2,1,0:T(8,128)}, u32[]{:S(2)}) copy-start(f32[96,4,8,128]{3,2,1,0:T(8,128)} %param.4) | copy-start | bytes 4718596
  61.3 2.8 copy-start.2
  111.5 26.8 %all-to-all-start = ((f32[96,8,512]{2,0,1:T(8,128)}), f32[96,8,512]{2,0,1:T(8,128)}, u32[]{:S(2)}, u32[]{:S(2)}) async-start(f32[96,8,512]{2,0,1:T(8,128)} %copy.15), calls=%async_computation | async-start | bytes 3145728 | tf_op jit(solution)/shard_map/all_to_all | solution.py:61
  117.6 301.2 %all-reduce.5.cloned.1.call-start = ((), (), s32[]{:S(2)}) async-start(), calls=%async_computation.3 | async-start | bytes 9437184 | tf_op jit(solution)/shard_map/psum | solution.py:63
  418.9 5.7 %copy-start.1 = (f32[768,768]{1,0:T(8,128)S(1)}, f32[768,768]{1,0:T(8,128)}, u32[]{:S(2)}) copy-start(f32[768,768]{1,0:T(8,128)} %get-tuple-element.9) | copy-start | bytes 7077892
Sparse Core Ops, SparseCore 0:
  145.2 273.5 all-reduce.4
where the time goes:
time: 555 us; the launch traced here: 554 us
  waiting for transfers between devices  311 us (56%)
  blocking collectives  102 us (18%)
  other arithmetic  60.9 us (11%)
  matrix products  24.2 us (4%)
  local copies, waits for them, and re-layouts  21.7 us (4%)
  starting transfers between devices  18.2 us (3%)
  between operations  16 us (3%)
    psum x1, waiting for transfers between devices, on_device(): lax.psum((highdot(cell_orbs, cell_orbs.T), highdot(cell_orbs, cell_images...  274 us
    psum x1, blocking collectives, on_device(): lax.psum((jnp.sum(grad * grad), jnp.sum(grad * prev_gradient), jnp.sum(pr...  74.7 us
    add x1, other arithmetic, on_device(): image = -0.5 * lap + potential[None] * orbitals  41.4 us
    all_to_all x1, blocking collectives, on_device(): lax.all_to_all(cell_grad, 'orb', split_axis=0, concat_axis=1, tiled=True)  27 us
    dot_general x4, matrix products, highdot(): jnp.dot(left, right, precision=lax.Precision.HIGHEST, preferred_element_t...  24.2 us
    ppermute x1, waiting for transfers between devices, padded_2(): lax.ppermute(tail, axis, [(i, (i + 1) % count) for i in range(ends)])  22.1 us
    all_to_all x1, waiting for transfers between devices, on_device(): lax.all_to_all(hmat_rows, 'orb', split_axis=1, concat_axis=0, tiled=True)  15.3 us
    concatenate x1, other arithmetic, padded_2(): jnp.concatenate([lax.ppermute(tail, axis, [(i, (i + 1) % count) for i in...  11.4 us
  transfers between devices with their start and end apart: 5, of which 4 were waited for; matrix products, arithmetic and copies ran while one was open for 13% of the time, Pallas kernels for 0%

commit v1 on v0

--- a/solution.py
+++ b/solution.py
@@ -60,8 +60,9 @@
         lax.all_to_all(cmat, "orb", split_axis=1, concat_axis=0, tiled=True),
         lax.all_to_all(hmat_rows, "orb", split_axis=1, concat_axis=0, tiled=True),
     )
-    correlation, hamilton = lax.psum(
-        (highdot(cell_orbs, cell_orbs.T), highdot(cell_orbs, cell_images.T)), ("orb", "dom")
+    correlation, hamilton = jax.lax.psum(
+        jax.lax.psum((highdot(cell_orbs, cell_orbs.T), highdot(cell_orbs, cell_images.T)), "orb"),
+        "dom",
     )
     correlation = correlation / cells
     hamilton = hamilton / cells

time: 555 us -> 532 us (0.959)
  waiting for transfers between devices: 311 us -> 290 us
    psum x1 -> x2, waiting for transfers between devices: 274 us -> 253 us  [the longest x1 172 us: on_device(): jax.lax.psum(jax.lax.psum((highdot(cell_orbs, cell_orbs.T), highdot(cell_...]
  transfers between devices with their start and end apart: 5 -> 6, of which waited for: 4 -> 5; matrix products, arithmetic and copies ran while one was open for 13% -> 13% of each run, Pallas kernels for 0% -> 0%
where the time goes in v1:
time: 532 us
  waiting for transfers between devices  290 us (55%)
  blocking collectives  100 us (19%)
  other arithmetic  60.7 us (11%)
  matrix products  24 us (5%)
  local copies, waits for them, and re-layouts  21.7 us (4%)
  starting transfers between devices  18.4 us (3%)
  between operations  16.1 us (3%)
    psum x1, waiting for transfers between devices, on_device(): jax.lax.psum(jax.lax.psum((highdot(cell_orbs, cell_orbs.T), highdot(cell_...  172 us
    psum x1, waiting for transfers between devices, on_device(): jax.lax.psum((highdot(cell_orbs, cell_orbs.T), highdot(cell_orbs, cell_im...  80.6 us
    psum x1, blocking collectives, on_device(): lax.psum((jnp.sum(grad * grad), jnp.sum(grad * prev_gradient), jnp.sum(pr...  74.2 us
    add x1, other arithmetic, on_device(): image = -0.5 * lap + potential[None] * orbitals  41.3 us
    all_to_all x1, blocking collectives, on_device(): lax.all_to_all(cell_grad, 'orb', split_axis=0, concat_axis=1, tiled=True)  26.2 us
    dot_general x4, matrix products, highdot(): jnp.dot(left, right, precision=lax.Precision.HIGHEST, preferred_element_t...  24 us
    ppermute x1, waiting for transfers between devices, padded_2(): lax.ppermute(tail, axis, [(i, (i + 1) % count) for i in range(ends)])  22.1 us
    all_to_all x1, waiting for transfers between devices, on_device(): lax.all_to_all(hmat_rows, 'orb', split_axis=1, concat_axis=0, tiled=True)  15.3 us
  transfers between devices with their start and end apart: 6, of which 5 were waited for; matrix products, arithmetic and copies ran while one was open for 13% of the time, Pallas kernels for 0%

profile of v1, /device:TPU:1, one launch (start us, length us, event | category | flops | bytes accessed | tf_op | source)
XLA Modules:
  0.0 531.6 jit_solution(4288899238009871594)
XLA Ops:
  7.2 5.5 %collective-permute-start.1 = (f32[96,4,8,128]{3,2,1,0:T(8,128)}, f32[96,4,8,128]{3,2,1,0:T(8,128)}, u32[]{:S(2)}, u32[]{:S(2)}) collective-permute-start(f32[96,4,8,128]{3,2,1,0:T(8,128)} %param.4), channel_id=1, source_target_pairs={{0,1},{1,2},{2,3},{3,4},{4,5},{5,6},{6,7},{7,8},{8,9},{9,10},{10,1... | collective-permute-start | bytes 4718600 | tf_op jit(solution)/shard_map/ppermute | solution.py:18
  15.5 2.1 copy.16
  17.5 5.3 all-to-all-start.1
  22.8 22.1 %collective-permute-done.1 = f32[96,4,8,128]{3,2,1,0:T(8,128)} collective-permute-done((f32[96,4,8,128]{3,2,1,0:T(8,128)}, f32[96,4,8,128]{3,2,1,0:T(8,128)}, u32[]{:S(2)}, u32[]{:S(2)}) %collective-permute-start.1) | collective-permute-done | bytes 1572896 | tf_op jit(solution)/shard_map/ppermute | solution.py:18
  44.9 2.7 constant_dynamic-update-slice_fusion.3
  47.6 2.1 constant_dynamic-update-slice_fusion.1
  49.9 11.4 %select_maximum_fusion = f32[96,12,16,136]{3,2,1,0:T(8,128)} fusion(f32[96,4,8,128]{3,2,1,0:T(8,128)} %collective-permute-done, f32[96,4,8,128]{3,2,1,0:T(8,128)S(1)} %copy-done, f32[96,4,8,128]{3,2,1,0:T(8,128)} %collective-permute-done.1), kind=kLoop, calls=%fused_computation.4 | loop fusion | flops 37601280 | bytes 14745600 | tf_op jit(solution)/shard_map/concatenate | solution.py:16
  61.3 2.7 constant_dynamic-update-slice_fusion
  64.0 41.3 %fusion.10 = f32[96,4,8,128]{3,2,1,0:T(8,128)} fusion(f32[96,12,16,136]{3,2,1,0:T(8,128)} %select_maximum_fusion, f32[96,8,8,128]{3,2,1,0:T(8,128)} %get-tuple-element.15, f32[96,8,8,128]{3,2,1,0:T(8,128)} %constant_dynamic-update-slice_fusion, f32[96,4,8,128]{3,2,1,0:T(8,128)S(1)} %copy-done, f32[96,4,8,128]{3,2,1,0:T(8,128)} %collective-permute-done, ...), kind=kLoop, calls=%fused_computation.18 | loop fusion | flops 15728640 | bytes 40910848 | tf_op jit(solution)/shard_map/add | solution.py:55
  105.3 2.6 all_to_all.40
  107.9 3.5 copy.15
  111.3 6.1 %all-to-all-start = ((f32[96,8,512]{2,0,1:T(8,128)}), f32[96,8,512]{2,0,1:T(8,128)}, u32[]{:S(2)}, u32[]{:S(2)}) async-start(f32[96,8,512]{2,0,1:T(8,128)} %copy.15), calls=%async_computation | async-start | bytes 3145728 | tf_op jit(solution)/shard_map/all_to_all | solution.py:61
  117.5 5.4 %fusion.38 = f32[768,768]{1,0:T(8,128)} fusion(f32[768,512]{1,0:T(8,128)S(1)} %bitcast.21), kind=kOutput, calls=%fused_computation.64 | convolution fusion | flops 3623878656 | bytes 3932160 | tf_op jit(solution)/shard_map/dot_general | solution.py:47
  122.9 15.3 %all-to-all-done = f32[96,8,512]{2,0,1:T(8,128)} async-done(((f32[96,8,512]{2,0,1:T(8,128)}), f32[96,8,512]{2,0,1:T(8,128)}, u32[]{:S(2)}, u32[]{:S(2)}) %all-to-all-start) | async-done | bytes 1572896 | tf_op jit(solution)/shard_map/all_to_all | solution.py:61
  138.1 6.8 %convolution_bitcast_fusion = f32[768,768]{1,0:T(8,128)} fusion(f32[768,512]{1,0:T(8,128)} %bitcast.1, f32[768,512]{1,0:T(8,128)S(1)} %bitcast.22), kind=kOutput, calls=%fused_computation.13 | convolution fusion | flops 3623878656 | bytes 5505024 | tf_op jit(solution)/shard_map/dot_general | solution.py:47
  145.2 80.6 %all-reduce.9.cloned.1.call-done = (f32[768,768]{1,0:T(8,128)}, f32[768,768]{1,0:T(8,128)}) async-done(((f32[768,768]{1,0:T(8,128)}, f32[768,768]{1,0:T(8,128)}), (f32[768,768]{1,0:T(8,128)}, f32[768,768]{1,0:T(8,128)})) %all-reduce.9.cloned.1.call-update) | async-done | bytes 4718608 | tf_op jit(solution)/shard_map/psum | solution.py:64
  225.8 172.2 %all-reduce.7.cloned.1.call-done = (f32[768,768]{1,0:T(8,128)}, f32[768,768]{1,0:T(8,128)}) async-done(((f32[768,768]{1,0:T(8,128)}, f32[768,768]{1,0:T(8,128)}), (f32[768,768]{1,0:T(8,128)}, f32[768,768]{1,0:T(8,128)})) %all-reduce.7.cloned.1.call-update) | async-done | bytes 4718608 | tf_op jit(solution)/shard_map/psum | solution.py:63
  398.0 5.7 %fusion.3 = f32[768,512]{1,0:T(8,128)S(1)} fusion(f32[768,512]{1,0:T(8,128)S(1)} %bitcast.23, f32[768,768]{1,0:T(8,128)} %get-tuple-element.8), kind=kOutput, calls=%fused_computation.9 | convolution fusion | flops 3624468480 | bytes 5505024 | tf_op jit(solution)/shard_map/dot_general | solution.py:47
  403.7 6.0 %multiply_subtract_fusion = f32[768,512]{1,0:T(8,128)S(1)} fusion(f32[768,512]{1,0:T(8,128)S(1)} %fusion.3, f32[768,512]{1,0:T(8,128)} %bitcast.1, f32[768,768]{1,0:T(8,128)S(1)} %copy-done.1), kind=kOutput, calls=%fused_computation.55 | convolution fusion | flops 3626434560 | bytes 7077888 | tf_op jit(solution)/shard_map/dot_general | solution.py:47
  409.8 26.2 %all_to_all.54 = f32[8,96,512]{2,1,0:T(8,128)S(1)} all-to-all(f32[8,96,512]{2,1,0:T(8,128)S(1)} %bitcast.25), channel_id=1, replica_groups=mesh['orb'=8,'dom'=32] {'orb'}, dimensions={0} | all-to-all | bytes 3145728 | tf_op jit(solution)/shard_map/all_to_all | solution.py:74
  438.1 2.4 reshape.24
  440.5 2.9 multiply_reduce_fusion
  444.4 74.2 %all-reduce.1 = (f32[]{:T(128)}, f32[]{:T(128)}, f32[]{:T(128)}) all-reduce(f32[]{:T(128)} %multiply_reduce_fusion.2, f32[]{:T(128)} %get-tuple-element.4, f32[]{:T(128)} %get-tuple-element.3), channel_id=1, replica_groups=mesh['orb'=8,'dom'=32] {'orb','dom'}, use_global_device_ids=true, to_apply=%region_5.6 | all-reduce | flops 3 | bytes 24 | tf_op jit(solution)/shard_map/psum | solution.py:76
  520.6 4.1 multiply_add_fusion
  (16 shorter events, 6.3 us)
Async XLA Ops:
  7.2 37.7 %collective-permute-start.1 = (f32[96,4,8,128]{3,2,1,0:T(8,128)}, f32[96,4,8,128]{3,2,1,0:T(8,128)}, u32[]{:S(2)}, u32[]{:S(2)}) collective-permute-start(f32[96,4,8,128]{3,2,1,0:T(8,128)} %param.4), channel_id=1, source_target_pairs={{0,1},{1,2},{2,3},{3,4},{4,5},{5,6},{6,7},{7,8},{8,9},{9,10},{10,1... | collective-permute-start | bytes 4718600 | tf_op jit(solution)/shard_map/ppermute | solution.py:18
  12.7 37.2 %collective-permute-start = (f32[96,4,8,128]{3,2,1,0:T(8,128)}, f32[96,4,8,128]{3,2,1,0:T(8,128)}, u32[]{:S(2)}, u32[]{:S(2)}) collective-permute-start(f32[96,4,8,128]{3,2,1,0:T(8,128)} %param.4), channel_id=1, source_target_pairs={{1,0},{2,1},{3,2},{4,3},{5,4},{6,5},{7,6},{8,7},{9,8},{10,9},{11,1... | collective-permute-start | bytes 4718600 | tf_op jit(solution)/shard_map/ppermute | solution.py:20
  17.5 93.8 %all-to-all-start.1 = ((f32[96,8,512]{2,0,1:T(8,128)}), f32[96,8,512]{2,0,1:T(8,128)S(1)}, u32[]{:S(2)}, u32[]{:S(2)}) async-start(f32[96,8,512]{2,0,1:T(8,128)} %copy.16), calls=%async_computation.1 | async-start | bytes 3145728 | tf_op jit(solution)/shard_map/all_to_all | solution.py:60
  22.8 24.8 %copy-start = (f32[96,4,8,128]{3,2,1,0:T(8,128)S(1)}, f32[96,4,8,128]{3,2,1,0:T(8,128)}, u32[]{:S(2)}) copy-start(f32[96,4,8,128]{3,2,1,0:T(8,128)} %param.4) | copy-start | bytes 4718596
  61.3 2.8 copy-start.2
  111.3 26.8 %all-to-all-start = ((f32[96,8,512]{2,0,1:T(8,128)}), f32[96,8,512]{2,0,1:T(8,128)}, u32[]{:S(2)}, u32[]{:S(2)}) async-start(f32[96,8,512]{2,0,1:T(8,128)} %copy.15), calls=%async_computation | async-start | bytes 3145728 | tf_op jit(solution)/shard_map/all_to_all | solution.py:61
  117.5 108.3 %all-reduce.9.cloned.1.call-start = ((), (), s32[]{:S(2)}) async-start(), calls=%async_computation.4 | async-start | bytes 9437184 | tf_op jit(solution)/shard_map/psum | solution.py:64
  145.0 253.0 %all-reduce.7.cloned.1.call-start = ((), (), s32[]{:S(2)}) async-start(), calls=%async_computation.3 | async-start | bytes 9437184 | tf_op jit(solution)/shard_map/psum | solution.py:63
  398.0 5.7 %copy-start.1 = (f32[768,768]{1,0:T(8,128)S(1)}, f32[768,768]{1,0:T(8,128)}, u32[]{:S(2)}) copy-start(f32[768,768]{1,0:T(8,128)} %get-tuple-element.9) | copy-start | bytes 7077892
Sparse Core Ops, SparseCore 0:
  145.1 80.6 all-reduce.8
  229.4 168.5 all-reduce.6
